TPU v7x, 256 devices: a whole 4x4x8 slice. The times are simulated.
256 devices in a mesh: expert: 32 (over z, y), etp: 8 (over x, core).
Axes of the slice: x: 4, y: 4, z: 8, core: 2. Of those that a mesh axis runs over, the one named last changes fastest.
Arguments:
- tokens: bfloat16 [32768, 2560], P(('expert', 'etp')), may hold values from -6 to 6
- grad_out: bfloat16 [32768, 2560], P(('expert', 'etp')), may hold values from -6 to 6
- router_weight: bfloat16 [2560, 32], replicated, may hold values from -0.125 to 0.125
- expert_choice: int32 [32768, 1], P(('expert', 'etp')), may hold values from 0 to 31; in each aligned block of 128 rows (0 to 127, 128 to 255, ...) at most 6 rows name the same one
- gate_pre: bfloat16 [32, 1536, 4096], P('expert', None, 'etp'), may hold values from -6 to 6
- up_pre: bfloat16 [32, 1536, 4096], P('expert', None, 'etp'), may hold values from -6 to 6
- w_gate: bfloat16 [32, 2560, 4096], P('expert', None, 'etp'), may hold values from -0.125 to 0.125
- w_up: bfloat16 [32, 2560, 4096], P('expert', None, 'etp'), may hold values from -0.125 to 0.125
- w_down: bfloat16 [32, 4096, 2560], P('expert', 'etp'), may hold values from -0.09375 to 0.09375
Outputs:
- token_grad: bfloat16 [32768, 2560], P(('expert', 'etp'))
- router_grad: float32 [2560, 32], replicated
Inputs may be any that keep to these rules, and one draw needn't show every extreme that they name: `expert_choice`: within the 128 tokens of one device no expert is chosen more than 6 times, and in every draw some expert is chosen exactly 6 times by the tokens of some device.
All inputs are finite; a program needn't handle non-finite values.
Results may differ from a plain program's by a relative error of at most 0.015.
Values may be sent and summed in bfloat16 or wider, within the bound.
No kernel may reach another device: no remote copies, remote signals or barrier semaphores. Data moves between devices by JAX's collectives and lax.ppermute only.
A program may use at most 128 MiB of HBM per device.

v0:
```python
import jax
import jax.numpy as jnp
from jax import lax
from jax.sharding import PartitionSpec as P


def local(tokens, grad_out, router_weight, expert_choice, gate_pre, up_pre, w_gate, w_up, w_down):
    width = tokens.shape[1]
    experts = router_weight.shape[1]
    n_expert = lax.axis_size("expert")
    n_etp = lax.axis_size("etp")
    capacity = gate_pre.shape[1] // (n_expert * n_etp)
    hidden = w_down.shape[1]
    contract = (((1,), (1,)), ((), ()))
    chosen_ids = expert_choice[:, 0]
    picked = chosen_ids[:, None] == jnp.arange(experts, dtype=jnp.int32)[None, :]
    logits = jnp.dot(tokens, router_weight, preferred_element_type=jnp.float32)
    score = jax.nn.sigmoid(jnp.sum(jnp.where(picked, logits, 0.0), axis=1))
    counts = picked.astype(jnp.int32)
    earlier = jnp.cumsum(counts, axis=0) - counts
    position = jnp.sum(earlier * counts, axis=1)
    target = chosen_ids * capacity + position
    outgoing = jnp.zeros((experts * capacity, width), jnp.bfloat16).at[target].set(grad_out)
    gate_all = gate_pre[0]
    up_all = up_pre[0]
    gate_w = w_gate[0]
    up_w = w_up[0]
    down_w = w_down[0]
    pooled = lax.all_gather(outgoing, "etp", axis=0, tiled=True)
    pooled = pooled.reshape(n_etp, experts * capacity, width)
    arrived = lax.all_to_all(pooled, "expert", split_axis=1, concat_axis=1, tiled=True)
    d_hidden = lax.dot_general(
        arrived.reshape(n_etp * experts * capacity, width),
        down_w,
        contract,
        preferred_element_type=jnp.float32,
    )
    gate_f = gate_all.astype(jnp.float32)
    up_f = up_all.astype(jnp.float32)
    sig = jax.nn.sigmoid(gate_f)
    d_gate = (d_hidden * up_f * sig * (1.0 + gate_f * (1.0 - sig))).astype(jnp.bfloat16)
    d_up = (d_hidden * gate_f * sig).astype(jnp.bfloat16)
    both = jnp.concatenate([d_gate, d_up], axis=1)
    term = lax.dot_general(both[:, :hidden], gate_w, contract, preferred_element_type=jnp.float32)
    terms = (
        term + lax.dot_general(both[:, hidden:], up_w, contract, preferred_element_type=jnp.float32)
    ).astype(jnp.bfloat16)
    terms = terms.reshape(n_etp, experts * capacity, width)
    swapped = lax.all_to_all(terms, "expert", split_axis=1, concat_axis=1, tiled=True)
    summed = lax.psum_scatter(swapped, "etp", scatter_dimension=0, tiled=True).astype(jnp.float32)
    returned = summed.reshape(experts * capacity, width).astype(jnp.bfloat16)
    fetched = returned[target].astype(jnp.float32)
    inputs = tokens.astype(jnp.float32)
    d_logit = jnp.sum(inputs * fetched, axis=1) * score * (1.0 - score)
    column = lax.dot_general(
        picked.astype(jnp.bfloat16), router_weight, contract, preferred_element_type=jnp.float32
    )
    token_grad = (score[:, None] * fetched + d_logit[:, None] * column).astype(jnp.bfloat16)
    weighted = jnp.where(picked, d_logit[:, None], 0.0)
    local_terms = jnp.dot(
        inputs.T, weighted, precision=lax.Precision.HIGHEST, preferred_element_type=jnp.float32
    )
    router_grad = lax.psum(local_terms, ("expert", "etp"))
    return (token_grad, router_grad)


def solution(mesh):
    placed = (
        P(("expert", "etp"), None),
        P(("expert", "etp"), None),
        P(),
        P(("expert", "etp"), None),
        P("expert", None, "etp"),
        P("expert", None, "etp"),
        P("expert", None, "etp"),
        P("expert", None, "etp"),
        P("expert", "etp", None),
    )
    return jax.shard_map(
        local,
        mesh=mesh,
        in_specs=placed,
        out_specs=(P(("expert", "etp"), None), P()),
        check_vma=False,
    )
```

profile of v0, /device:TPU:1, one launch (start us, length us, event | category | flops | bytes accessed | tf_op | source)
XLA Modules:
  0.0 812.3 jit_solution(2076231841087327123)
XLA Ops:
  7.2 0.0 copy-start
  7.2 0.0 all-gather.2.cloned.1.call-start
  7.2 0.8 fusion.28
  8.0 0.1 copy.20
  8.1 0.2 reduce_window_sum.11
  8.3 0.1 copy.21
  8.4 0.7 select_reduce_fusion
  9.1 0.7 fusion.33
  9.7 3.2 scatter_custom_fusion
  12.9 0.0 all-gather.2.cloned.1.call-update
  13.0 0.0 reduce-scatter.2.cloned.1.call-start
  13.0 54.4 %all-gather.2.cloned.1.call-done = bf16[1536,2560]{1,0:T(8,128)(2,1)} async-done(((bf16[192,2560]{1,0:T(8,128)(2,1)}), bf16[1536,2560]{1,0:T(8,128)(2,1)}) %all-gather.2.cloned.1.call-update) | async-done | bytes 7864336 | tf_op jit(solution)/shard_map/all_gather | solution.py:29
  67.4 10.7 %copy.22 = bf16[8,192,2560]{2,0,1:T(8,128)(2,1)} copy(bf16[8,192,2560]{2,1,0:T(8,128)(2,1)} %bitcast.44) | data formatting | bytes 15728640 | tf_op jit(solution)/shard_map/reshape | solution.py:30
  78.1 183.8 %all_to_all.10 = bf16[8,192,2560]{2,0,1:T(8,128)(2,1)} all-to-all(bf16[8,192,2560]{2,0,1:T(8,128)(2,1)} %copy.22), channel_id=1, replica_groups=mesh['expert'=32,'etp'=8] {'expert'}, dimensions={1} | all-to-all | bytes 15728640 | tf_op jit(solution)/shard_map/all_to_all | solution.py:31
  261.9 0.0 copy-start.5
  261.9 9.0 %copy.23 = bf16[8,192,2560]{2,1,0:T(8,128)(2,1)} copy(bf16[8,192,2560]{2,0,1:T(8,128)(2,1)} %all_to_all.10) | data formatting | bytes 15728640 | tf_op jit(solution)/shard_map/all_to_all | solution.py:31
  270.8 0.0 copy-done.5
  270.8 0.0 copy-start.6
  270.8 0.0 copy-start.7
  270.8 6.7 fusion.14
  277.6 0.0 copy-start.8
  277.6 1.7 copy-done.8
  279.3 0.0 copy-done
  279.3 0.0 copy-done.6
  279.3 0.0 copy-done.7
  279.3 9.9 %fusion.12 = f32[1536,2560]{1,0:T(8,128)} fusion(bf16[1,2560,512]{2,1,0:T(8,128)(2,1)S(1)} %copy-done, f32[1536,512]{1,0:T(8,128)S(1)} %fusion.14, bf16[1,1536,512]{2,1,0:T(8,128)(2,1)S(1)} %copy-done.6, bf16[1,1536,512]{2,1,0:T(8,128)(2,1)S(1)} %copy-done.7), kind=kOutput, calls=%fused_computation.21 | convolution fusion | flops 4035969024 | bytes 24641536 | tf_op jit(solution)/shard_map/dot_general | solution.py:44
  289.2 15.2 %add_convert_fusion = bf16[1536,2560]{1,0:T(8,128)(2,1)} fusion(f32[1536,2560]{1,0:T(8,128)} %fusion.12, bf16[1,2560,512]{2,1,0:T(8,128)(2,1)} %param.16, f32[1536,512]{1,0:T(8,128)} %copy-done.8, bf16[1,1536,512]{2,1,0:T(8,128)(2,1)} %param.13), kind=kOutput, calls=%fused_computation.2 | convolution fusion | flops 4039901184 | bytes 30932992 | tf_op jit(solution)/shard_map/dot_general | solution.py:46
  304.5 10.6 %copy.24 = bf16[8,192,2560]{2,0,1:T(8,128)(2,1)} copy(bf16[8,192,2560]{2,1,0:T(8,128)(2,1)} %bitcast.45) | data formatting | bytes 15728640 | tf_op jit(solution)/shard_map/reshape | solution.py:48
  315.1 177.6 %all_to_all.11 = bf16[8,192,2560]{2,0,1:T(8,128)(2,1)} all-to-all(bf16[8,192,2560]{2,0,1:T(8,128)(2,1)} %copy.24), channel_id=1, replica_groups=mesh['expert'=32,'etp'=8] {'expert'}, dimensions={1} | all-to-all | bytes 15728640 | tf_op jit(solution)/shard_map/all_to_all | solution.py:49
  492.6 8.7 %copy.25 = bf16[8,192,2560]{2,1,0:T(8,128)(2,1)} copy(bf16[8,192,2560]{2,0,1:T(8,128)(2,1)} %all_to_all.11) | data formatting | bytes 15728640 | tf_op jit(solution)/shard_map/all_to_all | solution.py:49
  501.4 0.0 copy-start.2
  501.4 0.0 copy-start.3
  501.4 0.0 copy-start.4
  501.4 0.0 reduce-scatter.2.cloned.1.call-update
  501.4 0.0 all-reduce.2.cloned.1.call-start
  501.5 1.0 copy-done.2
  502.5 0.0 copy-done.3
  502.5 0.0 copy-done.4
  502.5 0.3 fusion.24
  502.8 48.4 %reduce-scatter.2.cloned.1.call-done = bf16[1,192,2560]{2,1,0:T(8,128)(2,1)} async-done(((bf16[8,192,2560]{2,1,0:T(8,128)(2,1)}), bf16[1,192,2560]{2,1,0:T(8,128)(2,1)}) %reduce-scatter.2.cloned.1.call-update) | async-done | bytes 983056 | tf_op jit(solution)/shard_map/reduce_scatter | solution.py:50
  551.2 0.0 copy-start.1
  551.2 3.9 gather_fusion
  555.2 1.3 fusion.23
  556.5 1.1 convolution_bitcast_fusion
  557.7 0.0 all-reduce.2.cloned.1.call-update
  557.7 2.3 fusion.1
  560.0 244.0 %all-reduce.2.cloned.1.call-done = f32[2560,32]{0,1:T(8,128)} async-done(((f32[2560,32]{0,1:T(8,128)}), f32[2560,32]{0,1:T(8,128)}) %all-reduce.2.cloned.1.call-update) | async-done | bytes 327696 | tf_op jit(solution)/shard_map/psum | solution.py:63
  804.0 1.7 copy.27
  805.8 0.0 copy-done.1
  (2 shorter events, 0.0 us)
Async XLA Ops:
  7.2 272.1 %copy-start = (bf16[1,2560,512]{2,1,0:T(8,128)(2,1)S(1)}, bf16[1,2560,512]{2,1,0:T(8,128)(2,1)}, u32[]{:S(2)}) copy-start(bf16[1,2560,512]{2,1,0:T(8,128)(2,1)} %param.15) | copy-start | bytes 7864324
  7.2 60.2 %all-gather.2.cloned.1.call-start = ((), (), s32[]{:S(2)}) async-start(), calls=%async_computation.3 | async-start | bytes 8847360 | tf_op jit(solution)/shard_map/all_gather | solution.py:29
  13.0 538.3 %reduce-scatter.2.cloned.1.call-start = ((), (), s32[]{:S(2)}) async-start(), calls=%async_computation.4 | async-start | bytes 8847360 | tf_op jit(solution)/shard_map/reduce_scatter | solution.py:50
  261.9 9.0 %copy-start.5 = (bf16[1,512,2560]{2,1,0:T(8,128)(2,1)S(1)}, bf16[1,512,2560]{2,1,0:T(8,128)(2,1)}, u32[]{:S(2)}) copy-start(bf16[1,512,2560]{2,1,0:T(8,128)(2,1)} %param.17) | copy-start | bytes 7864324
  270.8 8.5 %copy-start.6 = (bf16[1,1536,512]{2,1,0:T(8,128)(2,1)S(1)}, bf16[1,1536,512]{2,1,0:T(8,128)(2,1)}, u32[]{:S(2)}) copy-start(bf16[1,1536,512]{2,1,0:T(8,128)(2,1)} %param.14) | copy-start | bytes 4718596
  270.8 8.5 %copy-start.7 = (bf16[1,1536,512]{2,1,0:T(8,128)(2,1)S(1)}, bf16[1,1536,512]{2,1,0:T(8,128)(2,1)}, u32[]{:S(2)}) copy-start(bf16[1,1536,512]{2,1,0:T(8,128)(2,1)} %param.13) | copy-start | bytes 4718596
  277.6 1.7 copy-start.8
  501.4 1.1 copy-start.2
  501.4 1.1 copy-start.3
  501.4 1.1 copy-start.4
  501.4 302.6 %all-reduce.2.cloned.1.call-start = ((), (), s32[]{:S(2)}) async-start(), calls=%async_computation.5 | async-start | bytes 655360 | tf_op jit(solution)/shard_map/psum | solution.py:63
  551.2 254.5 %copy-start.1 = (bf16[1,2560,512]{2,1,0:T(8,128)(2,1)S(1)}, bf16[1,2560,512]{2,1,0:T(8,128)(2,1)}, u32[]{:S(2)}) copy-start(bf16[1,2560,512]{2,1,0:T(8,128)(2,1)} %param.15) | copy-start | bytes 7864324
Sparse Core Ops, SparseCore 0:
  13.1 54.2 all-gather.1
  501.5 49.6 reduce-scatter.1
  557.8 246.1 all-reduce.1
where the time goes:
time: 813 us; the launch traced here: 812 us
  blocking collectives  361 us (44%)
  waiting for transfers between devices  347 us (43%)
  local copies, waits for them, and re-layouts  50.8 us (6%)
  matrix products  35.6 us (4%)
  between operations  13.8 us (2%)
    psum x1, waiting for transfers between devices, local(): router_grad = lax.psum(local_terms, ('expert', 'etp'))  244 us
    all_to_all x1, blocking collectives, local(): lax.all_to_all(pooled, 'expert', split_axis=1, concat_axis=1, tiled=True)  184 us
    all_to_all x1, blocking collectives, local(): lax.all_to_all(terms, 'expert', split_axis=1, concat_axis=1, tiled=True)  178 us
    all_gather x1, waiting for transfers between devices, local(): pooled = lax.all_gather(outgoing, 'etp', axis=0, tiled=True)  54.4 us
    reduce_scatter x1, waiting for transfers between devices, local(): lax.psum_scatter(swapped, 'etp', scatter_dimension=0, tiled=True)  48.4 us
  transfers between devices with their start and end apart: 3, of which 3 were waited for; matrix products, arithmetic and copies ran while one was open for 0% of the time, Pallas kernels for 0%

commit v1 on v0

--- a/solution.py
+++ b/solution.py
@@ -60,7 +60,9 @@
     local_terms = jnp.dot(
         inputs.T, weighted, precision=lax.Precision.HIGHEST, preferred_element_type=jnp.float32
     )
-    router_grad = lax.psum(local_terms, ("expert", "etp"))
+    router_grad = local_terms
+    for name in ("expert", "etp"):
+        router_grad = lax.psum(router_grad, name)
     return (token_grad, router_grad)
 
 

time: 813 us -> 776 us (0.954)
  waiting for transfers between devices: 347 us -> 309 us
    psum x1 -> x2, waiting for transfers between devices: 244 us -> 206 us  [local(): router_grad = lax.psum(router_grad, name)]
  transfers between devices with their start and end apart: 3 -> 4, of which waited for: 3 -> 4; matrix products, arithmetic and copies ran while one was open for 0% -> 0% of each run, Pallas kernels for 0% -> 0%
where the time goes in v1:
time: 776 us; the launch traced here: 774 us
  blocking collectives  361 us (47%)
  waiting for transfers between devices  309 us (40%)
  local copies, waits for them, and re-layouts  50.5 us (7%)
  matrix products  35.6 us (5%)
  between operations  13.8 us (2%)
    psum x2, waiting for transfers between devices, local(): router_grad = lax.psum(router_grad, name)  206 us
    all_to_all x1, blocking collectives, local(): lax.all_to_all(pooled, 'expert', split_axis=1, concat_axis=1, tiled=True)  184 us
    all_to_all x1, blocking collectives, local(): lax.all_to_all(terms, 'expert', split_axis=1, concat_axis=1, tiled=True)  178 us
    all_gather x1, waiting for transfers between devices, local(): pooled = lax.all_gather(outgoing, 'etp', axis=0, tiled=True)  54.4 us
    reduce_scatter x1, waiting for transfers between devices, local(): lax.psum_scatter(swapped, 'etp', scatter_dimension=0, tiled=True)  48.4 us
  transfers between devices with their start and end apart: 4, of which 4 were waited for; matrix products, arithmetic and copies ran while one was open for 0% of the time, Pallas kernels for 0%

profile of v1, /device:TPU:1, one launch (start us, length us, event | category | flops | bytes accessed | tf_op | source)
XLA Modules:
  0.0 774.2 jit_solution(5893750816429041148)
XLA Ops:
  7.2 0.0 copy-start
  7.2 0.0 all-gather.2.cloned.1.call-start
  7.2 0.8 fusion.28
  8.0 0.1 copy.20
  8.1 0.2 reduce_window_sum.11
  8.3 0.1 copy.21
  8.4 0.7 select_reduce_fusion
  9.1 0.7 fusion.33
  9.7 3.2 scatter_custom_fusion
  12.9 0.0 all-gather.2.cloned.1.call-update
  13.0 0.0 reduce-scatter.2.cloned.1.call-start
  13.0 54.4 %all-gather.2.cloned.1.call-done = bf16[1536,2560]{1,0:T(8,128)(2,1)} async-done(((bf16[192,2560]{1,0:T(8,128)(2,1)}), bf16[1536,2560]{1,0:T(8,128)(2,1)}) %all-gather.2.cloned.1.call-update) | async-done | bytes 7864336 | tf_op jit(solution)/shard_map/all_gather | solution.py:29
  67.4 10.7 %copy.22 = bf16[8,192,2560]{2,0,1:T(8,128)(2,1)} copy(bf16[8,192,2560]{2,1,0:T(8,128)(2,1)} %bitcast.44) | data formatting | bytes 15728640 | tf_op jit(solution)/shard_map/reshape | solution.py:30
  78.1 183.8 %all_to_all.10 = bf16[8,192,2560]{2,0,1:T(8,128)(2,1)} all-to-all(bf16[8,192,2560]{2,0,1:T(8,128)(2,1)} %copy.22), channel_id=1, replica_groups=mesh['expert'=32,'etp'=8] {'expert'}, dimensions={1} | all-to-all | bytes 15728640 | tf_op jit(solution)/shard_map/all_to_all | solution.py:31
  261.9 0.0 copy-start.5
  261.9 9.0 %copy.23 = bf16[8,192,2560]{2,1,0:T(8,128)(2,1)} copy(bf16[8,192,2560]{2,0,1:T(8,128)(2,1)} %all_to_all.10) | data formatting | bytes 15728640 | tf_op jit(solution)/shard_map/all_to_all | solution.py:31
  270.8 0.0 copy-done.5
  270.8 0.0 copy-start.6
  270.8 0.0 copy-start.7
  270.8 6.7 fusion.14
  277.6 0.0 copy-start.8
  277.6 1.7 copy-done.8
  279.3 0.0 copy-done
  279.3 0.0 copy-done.6
  279.3 0.0 copy-done.7
  279.3 9.9 %fusion.12 = f32[1536,2560]{1,0:T(8,128)} fusion(bf16[1,2560,512]{2,1,0:T(8,128)(2,1)S(1)} %copy-done, f32[1536,512]{1,0:T(8,128)S(1)} %fusion.14, bf16[1,1536,512]{2,1,0:T(8,128)(2,1)S(1)} %copy-done.6, bf16[1,1536,512]{2,1,0:T(8,128)(2,1)S(1)} %copy-done.7), kind=kOutput, calls=%fused_computation.21 | convolution fusion | flops 4035969024 | bytes 24641536 | tf_op jit(solution)/shard_map/dot_general | solution.py:44
  289.2 15.2 %add_convert_fusion = bf16[1536,2560]{1,0:T(8,128)(2,1)} fusion(f32[1536,2560]{1,0:T(8,128)} %fusion.12, bf16[1,2560,512]{2,1,0:T(8,128)(2,1)} %param.16, f32[1536,512]{1,0:T(8,128)} %copy-done.8, bf16[1,1536,512]{2,1,0:T(8,128)(2,1)} %param.13), kind=kOutput, calls=%fused_computation.2 | convolution fusion | flops 4039901184 | bytes 30932992 | tf_op jit(solution)/shard_map/dot_general | solution.py:46
  304.5 10.6 %copy.24 = bf16[8,192,2560]{2,0,1:T(8,128)(2,1)} copy(bf16[8,192,2560]{2,1,0:T(8,128)(2,1)} %bitcast.45) | data formatting | bytes 15728640 | tf_op jit(solution)/shard_map/reshape | solution.py:48
  315.1 177.6 %all_to_all.11 = bf16[8,192,2560]{2,0,1:T(8,128)(2,1)} all-to-all(bf16[8,192,2560]{2,0,1:T(8,128)(2,1)} %copy.24), channel_id=1, replica_groups=mesh['expert'=32,'etp'=8] {'expert'}, dimensions={1} | all-to-all | bytes 15728640 | tf_op jit(solution)/shard_map/all_to_all | solution.py:49
  492.6 8.7 %copy.25 = bf16[8,192,2560]{2,1,0:T(8,128)(2,1)} copy(bf16[8,192,2560]{2,0,1:T(8,128)(2,1)} %all_to_all.11) | data formatting | bytes 15728640 | tf_op jit(solution)/shard_map/all_to_all | solution.py:49
  501.4 0.0 copy-start.2
  501.4 0.0 copy-start.3
  501.4 0.0 copy-start.4
  501.4 0.0 reduce-scatter.2.cloned.1.call-update
  501.4 0.3 all-reduce.3.cloned.1.call-start
  501.7 0.7 copy-done.2
  502.5 0.0 copy-done.3
  502.5 0.0 copy-done.4
  502.5 0.3 fusion.24
  502.8 48.4 %reduce-scatter.2.cloned.1.call-done = bf16[1,192,2560]{2,1,0:T(8,128)(2,1)} async-done(((bf16[8,192,2560]{2,1,0:T(8,128)(2,1)}), bf16[1,192,2560]{2,1,0:T(8,128)(2,1)}) %reduce-scatter.2.cloned.1.call-update) | async-done | bytes 983056 | tf_op jit(solution)/shard_map/reduce_scatter | solution.py:50
  551.2 0.0 copy-start.1
  551.2 3.9 gather_fusion
  555.2 1.3 fusion.23
  556.5 1.1 convolution_bitcast_fusion
  557.7 0.0 all-reduce.3.cloned.1.call-update
  557.7 0.0 all-reduce.5.cloned.1.call-start
  557.7 140.7 %all-reduce.3.cloned.1.call-done = f32[2560,32]{0,1:T(8,128)} async-done(((f32[2560,32]{0,1:T(8,128)}), f32[2560,32]{0,1:T(8,128)}) %all-reduce.3.cloned.1.call-update) | async-done | bytes 327696 | tf_op jit(solution)/shard_map/psum | solution.py:65
  698.4 0.0 all-reduce.5.cloned.1.call-update
  698.4 2.3 fusion.1
  700.7 65.2 %all-reduce.5.cloned.1.call-done = f32[2560,32]{0,1:T(8,128)} async-done(((f32[2560,32]{0,1:T(8,128)}), f32[2560,32]{0,1:T(8,128)}) %all-reduce.5.cloned.1.call-update) | async-done | bytes 327696 | tf_op jit(solution)/shard_map/psum | solution.py:65
  765.9 1.7 copy.28
  767.6 0.0 copy-done.1
  (2 shorter events, 0.0 us)
Async XLA Ops:
  7.2 272.1 %copy-start = (bf16[1,2560,512]{2,1,0:T(8,128)(2,1)S(1)}, bf16[1,2560,512]{2,1,0:T(8,128)(2,1)}, u32[]{:S(2)}) copy-start(bf16[1,2560,512]{2,1,0:T(8,128)(2,1)} %param.15) | copy-start | bytes 7864324
  7.2 60.2 %all-gather.2.cloned.1.call-start = ((), (), s32[]{:S(2)}) async-start(), calls=%async_computation.3 | async-start | bytes 8847360 | tf_op jit(solution)/shard_map/all_gather | solution.py:29
  13.0 538.3 %reduce-scatter.2.cloned.1.call-start = ((), (), s32[]{:S(2)}) async-start(), calls=%async_computation.4 | async-start | bytes 8847360 | tf_op jit(solution)/shard_map/reduce_scatter | solution.py:50
  261.9 9.0 %copy-start.5 = (bf16[1,512,2560]{2,1,0:T(8,128)(2,1)S(1)}, bf16[1,512,2560]{2,1,0:T(8,128)(2,1)}, u32[]{:S(2)}) copy-start(bf16[1,512,2560]{2,1,0:T(8,128)(2,1)} %param.17) | copy-start | bytes 7864324
  270.8 8.5 %copy-start.6 = (bf16[1,1536,512]{2,1,0:T(8,128)(2,1)S(1)}, bf16[1,1536,512]{2,1,0:T(8,128)(2,1)}, u32[]{:S(2)}) copy-start(bf16[1,1536,512]{2,1,0:T(8,128)(2,1)} %param.14) | copy-start | bytes 4718596
  270.8 8.5 %copy-start.7 = (bf16[1,1536,512]{2,1,0:T(8,128)(2,1)S(1)}, bf16[1,1536,512]{2,1,0:T(8,128)(2,1)}, u32[]{:S(2)}) copy-start(bf16[1,1536,512]{2,1,0:T(8,128)(2,1)} %param.13) | copy-start | bytes 4718596
  277.6 1.7 copy-start.8
  501.4 1.1 copy-start.2
  501.4 1.1 copy-start.3
  501.4 1.1 copy-start.4
  501.4 197.0 %all-reduce.3.cloned.1.call-start = ((), (), s32[]{:S(2)}) async-start(), calls=%async_computation.5 | async-start | bytes 655360 | tf_op jit(solution)/shard_map/psum | solution.py:65
  551.2 216.4 %copy-start.1 = (bf16[1,2560,512]{2,1,0:T(8,128)(2,1)S(1)}, bf16[1,2560,512]{2,1,0:T(8,128)(2,1)}, u32[]{:S(2)}) copy-start(bf16[1,2560,512]{2,1,0:T(8,128)(2,1)} %param.15) | copy-start | bytes 7864324
  557.7 208.2 %all-reduce.5.cloned.1.call-start = ((), (), s32[]{:S(2)}) async-start(), calls=%async_computation.6 | async-start | bytes 655360 | tf_op jit(solution)/shard_map/psum | solution.py:65
Sparse Core Ops, SparseCore 0:
  13.1 54.2 all-gather.1
  501.5 49.6 reduce-scatter.1
  557.8 140.5 all-reduce.2
  700.7 65.1 all-reduce.4
